TPU v7x, 32 devices: a whole 2x2x4 slice. The times are simulated.
32 devices in a mesh: dp: 4 (over y, x), ctx: 2 (over core), tensor: 4 (over z).
Axes of the slice: x: 2, y: 2, z: 4, core: 2. Of those that a mesh axis runs over, the one named last changes fastest.
Arguments:
- inputs: bfloat16 [4, 1024, 2048], P('dp', 'ctx'), may hold values from -6 to 6
- segment_ids: int32 [4, 1024], P('dp', 'ctx'), may hold values from -1 to 1022, as said below
- attention_gain: float32 [2048], replicated, may hold values from 0.5 to 1.5
- query_weight: bfloat16 [2048, 2048], P(None, 'tensor'), may hold values from -0.125 to 0.125
- key_weight: bfloat16 [2048, 256], P(None, 'tensor'), may hold values from -0.125 to 0.125
- value_weight: bfloat16 [2048, 256], P(None, 'tensor'), may hold values from -0.125 to 0.125
- out_weight: bfloat16 [2048, 2048], P('tensor'), may hold values from -0.75 to 0.75
- feedforward_gain: float32 [2048], replicated, may hold values from 0.5 to 1.5
- gate_weight: bfloat16 [2048, 5632], P(None, 'tensor'), may hold values from -0.125 to 0.125
- up_weight: bfloat16 [2048, 5632], P(None, 'tensor'), may hold values from -0.125 to 0.125
- down_weight: bfloat16 [5632, 2048], P('tensor'), may hold values from -0.078125 to 0.078125
- cotangent: bfloat16 [4, 1024, 2048], P('dp', 'ctx'), may hold values from -6 to 6
Outputs:
- layer_out: bfloat16 [4, 1024, 2048], P('dp', 'ctx')
- grad_inputs: bfloat16 [4, 1024, 2048], P('dp', 'ctx')
- grad_attention_gain: float32 [2048], P(('dp', 'ctx'))
- grad_query_weight: float32 [2048, 2048], P(('dp', 'ctx'), 'tensor')
- grad_key_weight: float32 [2048, 256], P(('dp', 'ctx'), 'tensor')
- grad_value_weight: float32 [2048, 256], P(('dp', 'ctx'), 'tensor')
- grad_out_weight: float32 [2048, 2048], P('tensor', ('dp', 'ctx'))
- grad_feedforward_gain: float32 [2048], P(('dp', 'ctx'))
- grad_gate_weight: float32 [2048, 5632], P(('dp', 'ctx'), 'tensor')
- grad_up_weight: float32 [2048, 5632], P(('dp', 'ctx'), 'tensor')
- grad_down_weight: float32 [5632, 2048], P('tensor', ('dp', 'ctx'))
Inputs may be any that keep to these rules, and one draw needn't show every extreme that they name: `segment_ids`: along each sequence the numbers start at 0 and rise by at most one from token to token over the documents; the last 1 to 128 tokens of every sequence are padding, marked -1. In every draw the first sequence holds documents of one token each and a single padding token.
All inputs are finite; a program needn't handle non-finite values.
Results may differ from a plain program's by a relative error of at most 0.018.
Values may be sent and summed in bfloat16 or wider, within the bound.
A program may use at most 192 MiB of HBM per device.

v0:
```python
import math
import jax
import jax.numpy as jnp
from jax import lax
from jax.sharding import PartitionSpec as P

HEAD_DIM = 64
epsilon = 1e-05
rope_base = 10000.0
masked_score = -1e30


def positions_of(segment):
    token_index = jnp.arange(segment.shape[-1], dtype=jnp.int32)
    previous = jnp.concatenate([segment[..., :1] - 1, segment[..., :-1]], axis=-1)
    starts = jnp.where(segment != previous, token_index, 0)
    return token_index - lax.cummax(starts, axis=segment.ndim - 1)


def rotary_tables(positions):
    half_dim = HEAD_DIM // 2
    frequency = rope_base ** (-2.0 * jnp.arange(half_dim, dtype=jnp.float32) / HEAD_DIM)
    angles = positions.astype(jnp.float32)[..., None] * frequency
    return (jnp.cos(angles), jnp.sin(angles))


def rotate(values, cosine, sine_table):
    half_dim = values.shape[-1] // 2
    first = values[..., :half_dim]
    second = values[..., half_dim:]
    return jnp.concatenate(
        [first * cosine - second * sine_table, second * cosine + first * sine_table], axis=-1
    )


def visible(query_seg, key_seg, first_row):
    query_pos = first_row + jnp.arange(query_seg.shape[0], dtype=jnp.int32)
    key_pos = jnp.arange(key_seg.shape[0], dtype=jnp.int32)
    same_doc = query_seg[:, None] == key_seg[None, :]
    causal = key_pos[None, :] <= query_pos[:, None]
    usable = (key_seg[None, :] >= 0) | (key_pos[None, :] == query_pos[:, None])
    return same_doc & causal & usable


def body(
    inputs,
    segment_ids,
    attention_gain,
    query_weight,
    key_weight,
    value_weight,
    out_weight,
    feedforward_gain,
    gate_weight,
    up_weight,
    down_weight,
    cotangent,
):
    seq_count, span_len, model_width = inputs.shape
    row_count = seq_count * span_len
    query_heads = query_weight.shape[1] // HEAD_DIM
    kv_heads = key_weight.shape[1] // HEAD_DIM
    group_size = query_heads // kv_heads
    score_scale = 1.0 / math.sqrt(HEAD_DIM)
    offset = lax.axis_index("ctx") * span_len
    whole_segments = lax.all_gather(segment_ids, "ctx", axis=1, tiled=True)
    own_positions = lax.dynamic_slice_in_dim(positions_of(whole_segments), offset, span_len, 1)
    cosine, sine_table = rotary_tables(own_positions)
    cosine = cosine[:, :, None, :]
    sine_table = sine_table[:, :, None, :]
    hidden = inputs.astype(jnp.float32).reshape(row_count, model_width)
    inverse_one = lax.rsqrt(jnp.mean(hidden * hidden, axis=-1, keepdims=True) + epsilon)
    unit_one = hidden * inverse_one
    normed = (unit_one * attention_gain).astype(jnp.bfloat16)
    query_rows = rotate(
        jnp.dot(normed, query_weight, preferred_element_type=jnp.float32).reshape(
            seq_count, span_len, query_heads, HEAD_DIM
        ),
        cosine,
        sine_table,
    ).astype(jnp.bfloat16)
    key_rows = rotate(
        jnp.dot(normed, key_weight, preferred_element_type=jnp.float32).reshape(
            seq_count, span_len, kv_heads, HEAD_DIM
        ),
        cosine,
        sine_table,
    ).astype(jnp.bfloat16)
    value_rows = (
        jnp.dot(normed, value_weight, preferred_element_type=jnp.float32)
        .astype(jnp.bfloat16)
        .reshape(seq_count, span_len, kv_heads, HEAD_DIM)
    )
    all_keys, all_values = (
        lax.all_gather(key_rows, "ctx", axis=1, tiled=True),
        lax.all_gather(value_rows, "ctx", axis=1, tiled=True),
    )

    def attend(block_items):
        query_block, key_block, value_block, query_seg, key_seg = block_items
        allowed = visible(query_seg, key_seg, offset)
        grouped = query_block.reshape(span_len, kv_heads, group_size, HEAD_DIM)
        raw_scores = jnp.einsum(
            "qhgd,khd->hgqk", grouped, key_block, preferred_element_type=jnp.float32
        )
        scores = jnp.where(allowed, raw_scores * score_scale, masked_score)
        row_peak = jnp.max(scores, axis=-1, keepdims=True)
        shifted_exp = jnp.exp(scores - row_peak)
        denominator = jnp.sum(shifted_exp, axis=-1, keepdims=True)
        attn_probs = (shifted_exp / denominator).astype(jnp.bfloat16)
        mixed_block = jnp.einsum(
            "hgqk,khd->qhgd", attn_probs, value_block, preferred_element_type=jnp.float32
        )
        return (
            mixed_block.astype(jnp.bfloat16).reshape(span_len, query_heads * HEAD_DIM),
            row_peak + jnp.log(denominator),
        )

    mixed_heads, log_sums = lax.map(
        attend, (query_rows, all_keys, all_values, segment_ids, whole_segments)
    )
    mixed_flat = mixed_heads.reshape(row_count, query_heads * HEAD_DIM)
    attended = lax.psum(
        jnp.dot(mixed_flat, out_weight, preferred_element_type=jnp.float32), "tensor"
    )
    middle = hidden + attended
    inverse_two = lax.rsqrt(jnp.mean(middle * middle, axis=-1, keepdims=True) + epsilon)
    unit_two = middle * inverse_two
    normed_two = (unit_two * feedforward_gain).astype(jnp.bfloat16)
    gate_pre = jnp.dot(normed_two, gate_weight, preferred_element_type=jnp.float32)
    up_pre = jnp.dot(normed_two, up_weight, preferred_element_type=jnp.float32)
    sigmoid_gate = jax.nn.sigmoid(gate_pre)
    inner_act = (gate_pre * sigmoid_gate * up_pre).astype(jnp.bfloat16)
    feed_out = lax.psum(
        jnp.dot(inner_act, down_weight, preferred_element_type=jnp.float32).astype(jnp.bfloat16),
        "tensor",
    ).astype(jnp.float32)
    layer_out = (middle + feed_out).astype(jnp.bfloat16).reshape(seq_count, span_len, model_width)
    upstream = cotangent.reshape(row_count, model_width)
    grad_down = jnp.dot(inner_act.T, upstream, preferred_element_type=jnp.float32)
    grad_inner = jnp.dot(upstream, down_weight.T, preferred_element_type=jnp.float32)
    grad_up_pre = (grad_inner * gate_pre * sigmoid_gate).astype(jnp.bfloat16)
    grad_gate_pre = (
        grad_inner * up_pre * sigmoid_gate * (1.0 + gate_pre * (1.0 - sigmoid_gate))
    ).astype(jnp.bfloat16)
    grad_gate = jnp.dot(normed_two.T, grad_gate_pre, preferred_element_type=jnp.float32)
    grad_up = jnp.dot(normed_two.T, grad_up_pre, preferred_element_type=jnp.float32)
    grad_normed_two = lax.psum(
        jnp.dot(grad_gate_pre, gate_weight.T, preferred_element_type=jnp.float32)
        + jnp.dot(grad_up_pre, up_weight.T, preferred_element_type=jnp.float32),
        "tensor",
    )
    grad_ffn_gain = jnp.sum(grad_normed_two * unit_two, axis=0)
    scaled_two = grad_normed_two * feedforward_gain
    grad_middle = upstream.astype(jnp.float32) + inverse_two * (
        scaled_two - unit_two * jnp.mean(scaled_two * unit_two, axis=-1, keepdims=True)
    )
    grad_attended = grad_middle.astype(jnp.bfloat16)
    grad_out_part = jnp.dot(mixed_flat.T, grad_attended, preferred_element_type=jnp.float32)
    grad_mixed = (
        jnp.dot(grad_attended, out_weight.T, preferred_element_type=jnp.float32)
        .astype(jnp.bfloat16)
        .reshape(seq_count, span_len, query_heads, HEAD_DIM)
    )

    def attend_back(block_items):
        query_block, key_block, value_block, query_seg, key_seg, grad_block, log_block = block_items
        allowed = visible(query_seg, key_seg, offset)
        grouped = query_block.reshape(span_len, kv_heads, group_size, HEAD_DIM)
        grad_grouped = grad_block.reshape(span_len, kv_heads, group_size, HEAD_DIM)
        raw_scores = jnp.einsum(
            "qhgd,khd->hgqk", grouped, key_block, preferred_element_type=jnp.float32
        )
        scores = jnp.where(allowed, raw_scores * score_scale, masked_score)
        attn_probs = jnp.exp(scores - log_block)
        rounded = attn_probs.astype(jnp.bfloat16)
        grad_values = jnp.einsum(
            "hgqk,qhgd->khd", rounded, grad_grouped, preferred_element_type=jnp.float32
        )
        grad_probs = jnp.einsum(
            "qhgd,khd->hgqk", grad_grouped, value_block, preferred_element_type=jnp.float32
        )
        row_dot = jnp.sum(attn_probs * grad_probs, axis=-1, keepdims=True)
        grad_scores = (attn_probs * (grad_probs - row_dot) * score_scale).astype(jnp.bfloat16)
        grad_queries = jnp.einsum(
            "hgqk,khd->qhgd", grad_scores, key_block, preferred_element_type=jnp.float32
        ).reshape(span_len, query_heads, HEAD_DIM)
        grad_keys = jnp.einsum(
            "hgqk,qhgd->khd", grad_scores, grouped, preferred_element_type=jnp.float32
        )
        return (grad_queries, grad_keys, grad_values)

    grad_queries, grad_keys, grad_values = lax.map(
        attend_back,
        (query_rows, all_keys, all_values, segment_ids, whole_segments, grad_mixed, log_sums),
    )
    own_grad_keys, own_grad_values = (
        lax.psum_scatter(grad_keys, "ctx", scatter_dimension=1, tiled=True),
        lax.psum_scatter(grad_values, "ctx", scatter_dimension=1, tiled=True),
    )
    grad_query_pre = (
        rotate(grad_queries, cosine, -sine_table)
        .astype(jnp.bfloat16)
        .reshape(row_count, query_heads * HEAD_DIM)
    )
    grad_key_pre = (
        rotate(own_grad_keys, cosine, -sine_table)
        .astype(jnp.bfloat16)
        .reshape(row_count, kv_heads * HEAD_DIM)
    )
    grad_value_pre = own_grad_values.astype(jnp.bfloat16).reshape(row_count, kv_heads * HEAD_DIM)
    grad_query = jnp.dot(normed.T, grad_query_pre, preferred_element_type=jnp.float32)
    grad_key = jnp.dot(normed.T, grad_key_pre, preferred_element_type=jnp.float32)
    grad_value = jnp.dot(normed.T, grad_value_pre, preferred_element_type=jnp.float32)
    grad_normed = lax.psum(
        (
            jnp.dot(grad_query_pre, query_weight.T, preferred_element_type=jnp.float32)
            + jnp.dot(grad_key_pre, key_weight.T, preferred_element_type=jnp.float32)
            + jnp.dot(grad_value_pre, value_weight.T, preferred_element_type=jnp.float32)
        ).astype(jnp.bfloat16),
        "tensor",
    ).astype(jnp.float32)
    grad_attn_gain = jnp.sum(grad_normed * unit_one, axis=0)
    scaled_one = grad_normed * attention_gain
    grad_hidden = grad_middle + inverse_one * (
        scaled_one - unit_one * jnp.mean(scaled_one * unit_one, axis=-1, keepdims=True)
    )
    grad_inputs = grad_hidden.astype(jnp.bfloat16).reshape(seq_count, span_len, model_width)
    reduced = (
        lax.psum_scatter(
            grad_attn_gain.astype(jnp.bfloat16), ("dp", "ctx"), scatter_dimension=0, tiled=True
        ).astype(jnp.float32),
        lax.psum_scatter(
            grad_query.astype(jnp.bfloat16), ("dp", "ctx"), scatter_dimension=0, tiled=True
        ).astype(jnp.float32),
        lax.psum_scatter(
            grad_key.astype(jnp.bfloat16), ("dp", "ctx"), scatter_dimension=0, tiled=True
        ).astype(jnp.float32),
        lax.psum_scatter(
            grad_value.astype(jnp.bfloat16), ("dp", "ctx"), scatter_dimension=0, tiled=True
        ).astype(jnp.float32),
        lax.psum_scatter(
            grad_out_part.astype(jnp.bfloat16), ("dp", "ctx"), scatter_dimension=1, tiled=True
        ).astype(jnp.float32),
        lax.psum_scatter(
            grad_ffn_gain.astype(jnp.bfloat16), ("dp", "ctx"), scatter_dimension=0, tiled=True
        ).astype(jnp.float32),
        lax.psum_scatter(
            grad_gate.astype(jnp.bfloat16), ("dp", "ctx"), scatter_dimension=0, tiled=True
        ).astype(jnp.float32),
        lax.psum_scatter(
            grad_up.astype(jnp.bfloat16), ("dp", "ctx"), scatter_dimension=0, tiled=True
        ).astype(jnp.float32),
        lax.psum_scatter(
            grad_down.astype(jnp.bfloat16), ("dp", "ctx"), scatter_dimension=1, tiled=True
        ).astype(jnp.float32),
    )
    return (
        layer_out,
        grad_inputs,
        reduced[0],
        reduced[1],
        reduced[2],
        reduced[3],
        reduced[4],
        reduced[5],
        reduced[6],
        reduced[7],
        reduced[8],
    )


def solution(mesh):
    return jax.shard_map(
        body,
        mesh=mesh,
        in_specs=(
            P("dp", "ctx", None),
            P("dp", "ctx"),
            P(),
            P(None, "tensor"),
            P(None, "tensor"),
            P(None, "tensor"),
            P("tensor", None),
            P(),
            P(None, "tensor"),
            P(None, "tensor"),
            P("tensor", None),
            P("dp", "ctx", None),
        ),
        out_specs=(
            P("dp", "ctx", None),
            P("dp", "ctx", None),
            P(("dp", "ctx")),
            P(("dp", "ctx"), "tensor"),
            P(("dp", "ctx"), "tensor"),
            P(("dp", "ctx"), "tensor"),
            P("tensor", ("dp", "ctx")),
            P(("dp", "ctx")),
            P(("dp", "ctx"), "tensor"),
            P(("dp", "ctx"), "tensor"),
            P("tensor", ("dp", "ctx")),
        ),
        check_vma=False,
    )
```

profile of v0, /device:TPU:0, one launch (start us, length us, event | category | flops | bytes accessed | tf_op | source)
XLA Modules:
  0.0 1002.2 jit_solution(10803641659905566394)
XLA Ops:
  30.2 7.3 fusion.96
  37.5 8.0 fusion.4
  45.6 7.4 fusion.44
  56.6 157.4 %all-reduce.8.cloned.1.call-done = f32[512,2048]{1,0:T(8,128)} async-done(((f32[512,2048]{1,0:T(8,128)}), f32[512,2048]{1,0:T(8,128)}) %all-reduce.8.cloned.1.call-update) | async-done | bytes 4194320 | tf_op jit(solution)/shard_map/psum | solution.py:123
  218.0 10.1 %fusion.99 = f32[512,1408]{1,0:T(8,128)} fusion(bf16[512,2048]{1,0:T(8,128)(2,1)S(1)} %multiply_convert_fusion, bf16[2048,1408]{1,0:T(8,128)(2,1)} %param.21), kind=kOutput, calls=%fused_computation.149 | convolution fusion | flops 2952790016 | bytes 10747904 | tf_op jit(solution)/shard_map/dot_general | solution.py:131
  233.2 7.9 multiply_convert_fusion.1
  252.0 153.4 %all-reduce.10.cloned.1.call-done = f32[512,2048]{1,0:T(8,128)} async-done(((f32[512,2048]{1,0:T(8,128)}), f32[512,2048]{1,0:T(8,128)}) %all-reduce.10.cloned.1.call-update) | async-done | bytes 4194320 | tf_op jit(solution)/shard_map/psum | solution.py:148
  405.4 5.2 multiply_reduce_fusion
  410.6 5.3 multiply_add_fusion
  422.8 10.6 %fusion = (f32[8,512]{1,0:T(8,128)S(1)}, f32[1024,512,8]{1,0,2:T(8,128)}) fusion(f32[1,8,512,1024]{2,3,1,0:T(8,128)} %get-tuple-element.99, f32[8,512]{1,0:T(8,128)S(1)} %log_add_fusion, bf16[512,8,64]{0,2,1:T(8,128)(2,1)S(1)} %bitcast.196, bf16[1024,64]{0,1:T(8,128)(2,1)S(1)} %all-gather), kind=kOutput, calls=%fused_computation.3 | convolution fusion | flops 549449728 | bytes 34242560 | tf_op jit(solution)/shard_map/while/body/eval_jaxpr/qhgd,khd->hgqk/dot_general | solution.py:180
  433.5 12.1 %fusion.9 = bf16[8,512,1024]{1,2,0:T(8,128)(2,1)S(1)} fusion(f32[1024,512,8]{1,0,2:T(8,128)} %get-tuple-element.101, f32[1,8,512,1024]{2,3,1,0:T(8,128)} %get-tuple-element.99, f32[8,512]{1,0:T(8,128)S(1)} %get-tuple-element.100, f32[8,512]{1,0:T(8,128)S(1)} %log_add_fusion), kind=kLoop, calls=%fused_computation.14 | loop fusion | flops 20971520 | bytes 41975808 | tf_op jit(solution)/shard_map/reshape.65
  475.3 8.0 convolution_convert_fusion.1
  483.3 8.0 convolution_convert_fusion.2
  491.5 7.7 convolution_convert_fusion
  499.3 8.0 convolution_convert_fusion.5
  515.0 19.2 %reduce-scatter.16.cloned.1.call-done = bf16[256,64]{0,1:T(8,128)(2,1)} async-done(((bf16[2048,64]{0,1:T(8,128)(2,1)}), bf16[256,64]{0,1:T(8,128)(2,1)}) %reduce-scatter.16.cloned.1.call-update) | async-done | bytes 32784 | tf_op jit(solution)/shard_map/reduce_scatter | solution.py:236
  535.5 43.2 %reduce-scatter.20.cloned.1.call-done = bf16[512,256]{1,0:T(8,128)(2,1)} async-done(((bf16[512,2048]{1,0:T(8,128)(2,1)}), bf16[512,256]{1,0:T(8,128)(2,1)}) %reduce-scatter.20.cloned.1.call-update) | async-done | bytes 262160 | tf_op jit(solution)/shard_map/reduce_scatter | solution.py:242
  580.5 43.1 %reduce-scatter.14.cloned.1.call-done = bf16[256,512]{1,0:T(8,128)(2,1)} async-done(((bf16[2048,512]{1,0:T(8,128)(2,1)}), bf16[256,512]{1,0:T(8,128)(2,1)}) %reduce-scatter.14.cloned.1.call-update) | async-done | bytes 262160 | tf_op jit(solution)/shard_map/reduce_scatter | solution.py:233
  625.4 60.7 %reduce-scatter.24.cloned.1.call-done = bf16[256,1408]{1,0:T(8,128)(2,1)} async-done(((bf16[2048,1408]{1,0:T(8,128)(2,1)}), bf16[256,1408]{1,0:T(8,128)(2,1)}) %reduce-scatter.24.cloned.1.call-update) | async-done | bytes 720912 | tf_op jit(solution)/shard_map/reduce_scatter | solution.py:251
  688.5 60.4 %reduce-scatter.22.cloned.1.call-done = bf16[256,1408]{1,0:T(8,128)(2,1)} async-done(((bf16[2048,1408]{1,0:T(8,128)(2,1)}), bf16[256,1408]{1,0:T(8,128)(2,1)}) %reduce-scatter.22.cloned.1.call-update) | async-done | bytes 720912 | tf_op jit(solution)/shard_map/reduce_scatter | solution.py:248
  751.2 60.2 %reduce-scatter.26.cloned.1.call-done = bf16[1408,256]{1,0:T(8,128)(2,1)} async-done(((bf16[1408,2048]{1,0:T(8,128)(2,1)}), bf16[1408,256]{1,0:T(8,128)(2,1)}) %reduce-scatter.26.cloned.1.call-update) | async-done | bytes 720912 | tf_op jit(solution)/shard_map/reduce_scatter | solution.py:254
  813.8 156.0 %all-reduce.12.cloned.1.call-done = (bf16[512,2048]{1,0:T(8,128)(2,1)}, bf16[512,2048]{1,0:T(8,128)(2,1)}) async-done(((bf16[512,2048]{1,0:T(8,128)(2,1)}, bf16[512,2048]{1,0:T(8,128)(2,1)}), (bf16[512,2048]{1,0:T(8,128)(2,1)}, bf16[512,2048]{1,0:T(8,128)(2,1)})) %all-reduce.12.cloned.1.call-update) | async-done | bytes 4194320 | tf_op jit(solution)/shard_map/psum | solution.py:134
  972.7 13.9 %all-reduce.2 = (bf16[2048]{0:T(1024)(128)(2,1)S(1)}, bf16[2048]{0:T(1024)(128)(2,1)S(1)}) all-reduce(bf16[2048]{0:T(1024)(128)(2,1)S(1)} %get-tuple-element.64, bf16[2048]{0:T(1024)(128)(2,1)S(1)} %copy-done.28), channel_id=5, replica_groups=mesh['dp'=4,'ctx'=2,'tensor'=4] {'dp','ctx'}, use_global_device_ids=true, to_apply=%region_16.17.clone | all-reduce | flops 4096 | bytes 16384
  986.7 7.8 fusion.29
  (178 shorter events, 104.8 us)
Async XLA Ops:
  7.2 45.8 %copy-start = (bf16[512,2048]{1,0:T(8,128)(2,1)S(1)}, bf16[512,2048]{1,0:T(8,128)(2,1)}, u32[]{:S(2)}) copy-start(bf16[512,2048]{1,0:T(8,128)(2,1)} %param.18) | copy-start | bytes 6291460
  7.2 10.8 %copy-start.22 = (f32[2048]{0:T(1024)S(1)}, f32[2048]{0:T(1024)}, u32[]{:S(2)}) copy-start(f32[2048]{0:T(1024)} %param.14) | copy-start | bytes 24580
  7.2 206.8 %all-reduce.8.cloned.1.call-start = ((), (), s32[]{:S(2)}) async-start(), calls=%async_computation.9 | async-start | bytes 8388608 | tf_op jit(solution)/shard_map/psum | solution.py:123
  7.3 12.0 %copy-start.30 = (f32[32]{0:T(128)}, f32[32]{0:T(128)S(1)}, u32[]{:S(2)}) copy-start(f32[32]{0:T(128)S(1)} %multiply_power_fusion) | copy-start | bytes 388
  12.1 13.3 %copy-start.26 = (f32[512]{0:T(512)}, f32[512]{0:T(512)S(1)}, u32[]{:S(2)}) copy-start(f32[512]{0:T(512)S(1)} %add_rsqrt_fusion.1) | copy-start | bytes 6148
  56.3 161.2 %copy-start.18 = (f32[2048]{0:T(1024)S(1)}, f32[2048]{0:T(1024)}, u32[]{:S(2)}) copy-start(f32[2048]{0:T(1024)} %param.19) | copy-start | bytes 24580
  56.4 349.1 %all-reduce.10.cloned.1.call-start = ((), (), s32[]{:S(2)}) async-start(), calls=%async_computation.10 | async-start | bytes 8388608 | tf_op jit(solution)/shard_map/psum | solution.py:148
  218.0 15.2 %slice-start.8 = ((s8[5767168]{0:T(1024)(128)(4,1)}), s8[4194304]{0:T(1024)(128)(4,1)S(1)}, s32[]{:S(2)}) async-start(s8[5767168]{0:T(1024)(128)(4,1)} %bitcast.214), calls=%async_computation.29 | async-start | bytes 8388608
  228.1 17.9 %slice-start.6 = ((s8[5767168]{0:T(1024)(128)(4,1)}), s8[4194304]{0:T(1024)(128)(4,1)S(1)}, s32[]{:S(2)}) async-start(s8[5767168]{0:T(1024)(128)(4,1)} %bitcast.212), calls=%async_computation.27 | async-start | bytes 8388608
  233.2 12.9 %slice-start.7 = ((s8[5767168]{0:T(1024)(128)(4,1)}), s8[1572864]{0:T(1024)(128)(4,1)S(1)}, s32[]{:S(2)}) async-start(s8[5767168]{0:T(1024)(128)(4,1)} %bitcast.212), calls=%async_computation.28 | async-start | bytes 3145728
  251.2 154.2 %copy-start.19 = (f32[2048]{0:T(1024)S(1)}, f32[2048]{0:T(1024)}, u32[]{:S(2)}) copy-start(f32[2048]{0:T(1024)} %param.19) | copy-start | bytes 24580
  251.3 201.1 %reduce-scatter.12.cloned.1.call-start = ((), (), s32[]{:S(2)}) async-start(), calls=%async_computation.12 | async-start | bytes 393216 | tf_op jit(solution)/shard_map/reduce_scatter | solution.py:199
  405.4 13.8 %slice-start = ((s8[16777216]{0:T(1024)(128)(4,1)}), s8[4194304]{0:T(1024)(128)(4,1)S(1)}, s32[]{:S(2)}) async-start(s8[16777216]{0:T(1024)(128)(4,1)} %bitcast.191), calls=%async_computation.21 | async-start | bytes 8388608
  405.4 13.8 %slice-start.1 = ((s8[16777216]{0:T(1024)(128)(4,1)}), s8[4194304]{0:T(1024)(128)(4,1)S(1)}, s32[]{:S(2)}) async-start(s8[16777216]{0:T(1024)(128)(4,1)} %bitcast.191), calls=%async_computation.22 | async-start | bytes 8388608
  433.4 25.7 %reduce-scatter.10.cloned.1.call-start = ((), (), s32[]{:S(2)}) async-start(), calls=%async_computation.11 | async-start | bytes 393216 | tf_op jit(solution)/shard_map/reduce_scatter | solution.py:198
  452.3 61.3 %reduce-scatter.18.cloned.1.call-start = ((), (), s32[]{:S(2)}) async-start(), calls=%async_computation.15 | async-start | bytes 294912 | tf_op jit(solution)/shard_map/reduce_scatter | solution.py:239
  454.8 79.4 %reduce-scatter.16.cloned.1.call-start = ((), (), s32[]{:S(2)}) async-start(), calls=%async_computation.14 | async-start | bytes 294912 | tf_op jit(solution)/shard_map/reduce_scatter | solution.py:236
  461.8 116.9 %reduce-scatter.20.cloned.1.call-start = ((), (), s32[]{:S(2)}) async-start(), calls=%async_computation.16 | async-start | bytes 2359296 | tf_op jit(solution)/shard_map/reduce_scatter | solution.py:242
  466.7 157.0 %reduce-scatter.14.cloned.1.call-start = ((), (), s32[]{:S(2)}) async-start(), calls=%async_computation.13 | async-start | bytes 2359296 | tf_op jit(solution)/shard_map/reduce_scatter | solution.py:233
  475.2 211.0 %reduce-scatter.24.cloned.1.call-start = ((), (), s32[]{:S(2)}) async-start(), calls=%async_computation.18 | async-start | bytes 6488064 | tf_op jit(solution)/shard_map/reduce_scatter | solution.py:251
  483.3 265.7 %reduce-scatter.22.cloned.1.call-start = ((), (), s32[]{:S(2)}) async-start(), calls=%async_computation.17 | async-start | bytes 6488064 | tf_op jit(solution)/shard_map/reduce_scatter | solution.py:248
  491.3 320.2 %reduce-scatter.26.cloned.1.call-start = ((), (), s32[]{:S(2)}) async-start(), calls=%async_computation.19 | async-start | bytes 6488064 | tf_op jit(solution)/shard_map/reduce_scatter | solution.py:254
  499.3 470.5 %all-reduce.12.cloned.1.call-start = ((), (), s32[]{:S(2)}) async-start(), calls=%async_computation.20 | async-start | bytes 8388608 | tf_op jit(solution)/shard_map/psum | solution.py:134
  688.5 284.2 %copy-start.28 = (bf16[2048]{0:T(1024)(128)(2,1)S(1)}, bf16[2048]{0:T(1024)(128)(2,1)}, u32[]{:S(2)}) copy-start(bf16[2048]{0:T(1024)(128)(2,1)} %get-tuple-element.62) | copy-start | bytes 12292
  (32 other events, 182.4 us)
Sparse Core Ops, SparseCore 0:
  56.5 157.5 all-reduce.7
  251.4 153.9 all-reduce.9
  433.5 6.6 reduce-scatter.11
  452.4 6.6 reduce-scatter.9
  461.9 34.7 reduce-scatter.17
  500.5 33.5 reduce-scatter.15
  537.4 41.2 reduce-scatter.19
  582.3 41.2 reduce-scatter.13
  627.1 59.0 reduce-scatter.23
  689.9 59.0 reduce-scatter.21
  752.4 59.0 reduce-scatter.25
  814.4 155.3 all-reduce.11
where the time goes:
time: 1010 us; the launch traced here: 1000 us
  waiting for transfers between devices  758 us (75%)
  matrix products  129 us (13%)
  other arithmetic  65 us (6%)
  blocking collectives  19.9 us (2%)
  between operations  16.3 us (2%)
  local copies, waits for them, and re-layouts  12.1 us (1%)
    psum x1, waiting for transfers between devices, body(): lax.psum(jnp.dot(mixed_flat, out_weight, preferred_element_type=jnp.float...  157 us
    psum x1, waiting for transfers between devices, body(): lax.psum(jnp.dot(inner_act, down_weight, preferred_element_type=jnp.float...  156 us
    psum x1, waiting for transfers between devices, body(): lax.psum(jnp.dot(grad_gate_pre, gate_weight.T, preferred_element_type=jnp...  153 us
    reduce_scatter x1, waiting for transfers between devices, body(): lax.psum_scatter(grad_up.astype(jnp.bfloat16), ('dp', 'ctx'), scatter_dim...  60.7 us
    reduce_scatter x1, waiting for transfers between devices, body(): lax.psum_scatter(grad_gate.astype(jnp.bfloat16), ('dp', 'ctx'), scatter_d...  60.4 us
    reduce_scatter x1, waiting for transfers between devices, body(): lax.psum_scatter(grad_down.astype(jnp.bfloat16), ('dp', 'ctx'), scatter_d...  60.2 us
    reduce_scatter x1, waiting for transfers between devices, body(): lax.psum_scatter(grad_out_part.astype(jnp.bfloat16), ('dp', 'ctx'), scatt...  43.2 us
    reduce_scatter x1, waiting for transfers between devices, body(): lax.psum_scatter(grad_query.astype(jnp.bfloat16), ('dp', 'ctx'), scatter_...  43.1 us
  transfers between devices with their start and end apart: 12, of which 10 were waited for; matrix products, arithmetic and copies ran while one was open for 8% of the time, Pallas kernels for 0%

commit v1 on v0

--- a/solution.py
+++ b/solution.py
@@ -145,10 +145,13 @@
     ).astype(jnp.bfloat16)
     grad_gate = jnp.dot(normed_two.T, grad_gate_pre, preferred_element_type=jnp.float32)
     grad_up = jnp.dot(normed_two.T, grad_up_pre, preferred_element_type=jnp.float32)
-    grad_normed_two = lax.psum(
-        jnp.dot(grad_gate_pre, gate_weight.T, preferred_element_type=jnp.float32)
-        + jnp.dot(grad_up_pre, up_weight.T, preferred_element_type=jnp.float32),
-        "tensor",
+    grad_normed_two = jnp.sum(
+        lax.all_gather(
+            jnp.dot(grad_gate_pre, gate_weight.T, preferred_element_type=jnp.float32)
+            + jnp.dot(grad_up_pre, up_weight.T, preferred_element_type=jnp.float32),
+            "tensor",
+        ),
+        axis=0,
     )
     grad_ffn_gain = jnp.sum(grad_normed_two * unit_two, axis=0)
     scaled_two = grad_normed_two * feedforward_gain

time: 1010 us -> 1150 us (1.14)
  waiting for transfers between devices: 758 us -> 890 us
    all_gather x0 -> x1, waiting for transfers between devices: none -> 286 us  [body(): lax.all_gather(jnp.dot(grad_gate_pre, gate_weight.T, preferred_element_ty...]
    psum x1 -> x0, waiting for transfers between devices: 153 us -> none  [body(): lax.psum(jnp.dot(grad_gate_pre, gate_weight.T, preferred_element_type=jnp...]
    reduce_scatter x1, waiting for transfers between devices: 60.7 us -> 13 us  [body(): lax.psum_scatter(grad_up.astype(jnp.bfloat16), ('dp', 'ctx'), scatter_dim...]
    reduce_scatter x1, waiting for transfers between devices: 0.02 us -> 34.4 us  [body(): lax.psum_scatter(grad_value.astype(jnp.bfloat16), ('dp', 'ctx'), scatter_...]
    reduce_scatter x1, waiting for transfers between devices: 19.2 us -> 36.2 us  [body(): lax.psum_scatter(grad_key.astype(jnp.bfloat16), ('dp', 'ctx'), scatter_di...]
  transfers between devices with their start and end apart: 12 -> 12, of which waited for: 10 -> 10; matrix products, arithmetic and copies ran while one was open for 8% -> 7% of each run, Pallas kernels for 0% -> 0%
where the time goes in v1:
time: 1150 us; the launch traced here: 1140 us
  waiting for transfers between devices  890 us (77%)
  matrix products  126 us (11%)
  other arithmetic  75.4 us (7%)
  blocking collectives  19.9 us (2%)
  between operations  16.3 us (1%)
  local copies, waits for them, and re-layouts  14.9 us (1%)
    all_gather x1, waiting for transfers between devices, body(): lax.all_gather(jnp.dot(grad_gate_pre, gate_weight.T, preferred_element_ty...  286 us
    psum x1, waiting for transfers between devices, body(): lax.psum(jnp.dot(mixed_flat, out_weight, preferred_element_type=jnp.float...  157 us
    psum x1, waiting for transfers between devices, body(): lax.psum(jnp.dot(inner_act, down_weight, preferred_element_type=jnp.float...  156 us
    reduce_scatter x1, waiting for transfers between devices, body(): lax.psum_scatter(grad_down.astype(jnp.bfloat16), ('dp', 'ctx'), scatter_d...  60.6 us
    reduce_scatter x1, waiting for transfers between devices, body(): lax.psum_scatter(grad_gate.astype(jnp.bfloat16), ('dp', 'ctx'), scatter_d...  60.1 us
    reduce_scatter x1, waiting for transfers between devices, body(): lax.psum_scatter(grad_query.astype(jnp.bfloat16), ('dp', 'ctx'), scatter_...  43.1 us
    reduce_scatter x1, waiting for transfers between devices, body(): lax.psum_scatter(grad_out_part.astype(jnp.bfloat16), ('dp', 'ctx'), scatt...  43 us
    reduce_scatter x1, waiting for transfers between devices, body(): lax.psum_scatter(grad_key.astype(jnp.bfloat16), ('dp', 'ctx'), scatter_di...  36.2 us
  transfers between devices with their start and end apart: 12, of which 10 were waited for; matrix products, arithmetic and copies ran while one was open for 7% of the time, Pallas kernels for 0%

profile of v1, /device:TPU:0, one launch (start us, length us, event | category | flops | bytes accessed | tf_op | source)
XLA Modules:
  0.0 1143.7 jit_solution(14019382628078651320)
XLA Ops:
  30.8 7.3 fusion.96
  38.1 8.0 fusion.4
  46.1 7.4 fusion.44
  57.1 157.4 %all-reduce.7.cloned.1.call-done = f32[512,2048]{1,0:T(8,128)} async-done(((f32[512,2048]{1,0:T(8,128)}), f32[512,2048]{1,0:T(8,128)}) %all-reduce.7.cloned.1.call-update) | async-done | bytes 4194320 | tf_op jit(solution)/shard_map/psum | solution.py:123
  218.5 10.1 fusion.99
  233.8 7.9 multiply_convert_fusion.1
  252.1 285.7 %all-gather.4.cloned.1.call-done = f32[2048,2048]{1,0:T(8,128)} async-done(((f32[512,2048]{1,0:T(8,128)}), f32[2048,2048]{1,0:T(8,128)}) %all-gather.4.cloned.1.call-update) | async-done | bytes 16777232 | tf_op jit(solution)/shard_map/all_gather | solution.py:149
  537.8 10.2 reduce_sum.86
  565.0 10.6 fusion
  575.6 12.1 %fusion.9 = bf16[8,512,1024]{1,2,0:T(8,128)(2,1)S(1)} fusion(f32[1024,512,8]{1,0,2:T(8,128)} %get-tuple-element.101, f32[1,8,512,1024]{2,3,1,0:T(8,128)} %get-tuple-element.99, f32[8,512]{1,0:T(8,128)S(1)} %get-tuple-element.100, f32[8,512]{1,0:T(8,128)S(1)} %log_add_fusion), kind=kLoop, calls=%fused_computation.14 | loop fusion | flops 20971520 | bytes 41975808 | tf_op jit(solution)/shard_map/reshape.65
  594.9 6.6 convolution_convert_fusion.1
  601.6 6.7 convolution_convert_fusion.2
  609.9 6.8 convolution_convert_fusion
  637.1 8.0 convolution_convert_fusion.5
  651.4 13.0 %reduce-scatter.24.cloned.1.call-done = bf16[256,1408]{1,0:T(8,128)(2,1)} async-done(((bf16[2048,1408]{1,0:T(8,128)(2,1)}), bf16[256,1408]{1,0:T(8,128)(2,1)}) %reduce-scatter.24.cloned.1.call-update) | async-done | bytes 720912 | tf_op jit(solution)/shard_map/reduce_scatter | solution.py:254
  666.6 60.1 %reduce-scatter.22.cloned.1.call-done = bf16[256,1408]{1,0:T(8,128)(2,1)} async-done(((bf16[2048,1408]{1,0:T(8,128)(2,1)}), bf16[256,1408]{1,0:T(8,128)(2,1)}) %reduce-scatter.22.cloned.1.call-update) | async-done | bytes 720912 | tf_op jit(solution)/shard_map/reduce_scatter | solution.py:251
  729.0 60.6 %reduce-scatter.26.cloned.1.call-done = bf16[1408,256]{1,0:T(8,128)(2,1)} async-done(((bf16[1408,2048]{1,0:T(8,128)(2,1)}), bf16[1408,256]{1,0:T(8,128)(2,1)}) %reduce-scatter.26.cloned.1.call-update) | async-done | bytes 720912 | tf_op jit(solution)/shard_map/reduce_scatter | solution.py:257
  791.9 34.4 %reduce-scatter.18.cloned.1.call-done = bf16[256,64]{0,1:T(8,128)(2,1)} async-done(((bf16[2048,64]{0,1:T(8,128)(2,1)}), bf16[256,64]{0,1:T(8,128)(2,1)}) %reduce-scatter.18.cloned.1.call-update) | async-done | bytes 32784 | tf_op jit(solution)/shard_map/reduce_scatter | solution.py:242
  827.7 36.2 %reduce-scatter.16.cloned.1.call-done = bf16[256,64]{0,1:T(8,128)(2,1)} async-done(((bf16[2048,64]{0,1:T(8,128)(2,1)}), bf16[256,64]{0,1:T(8,128)(2,1)}) %reduce-scatter.16.cloned.1.call-update) | async-done | bytes 32784 | tf_op jit(solution)/shard_map/reduce_scatter | solution.py:239
  865.3 43.0 %reduce-scatter.20.cloned.1.call-done = bf16[512,256]{1,0:T(8,128)(2,1)} async-done(((bf16[512,2048]{1,0:T(8,128)(2,1)}), bf16[512,256]{1,0:T(8,128)(2,1)}) %reduce-scatter.20.cloned.1.call-update) | async-done | bytes 262160 | tf_op jit(solution)/shard_map/reduce_scatter | solution.py:245
  910.0 43.1 %reduce-scatter.14.cloned.1.call-done = bf16[256,512]{1,0:T(8,128)(2,1)} async-done(((bf16[2048,512]{1,0:T(8,128)(2,1)}), bf16[256,512]{1,0:T(8,128)(2,1)}) %reduce-scatter.14.cloned.1.call-update) | async-done | bytes 262160 | tf_op jit(solution)/shard_map/reduce_scatter | solution.py:236
  954.9 156.4 %all-reduce.9.cloned.1.call-done = (bf16[512,2048]{1,0:T(8,128)(2,1)}, bf16[512,2048]{1,0:T(8,128)(2,1)}) async-done(((bf16[512,2048]{1,0:T(8,128)(2,1)}, bf16[512,2048]{1,0:T(8,128)(2,1)}), (bf16[512,2048]{1,0:T(8,128)(2,1)}, bf16[512,2048]{1,0:T(8,128)(2,1)})) %all-reduce.9.cloned.1.call-update) | async-done | bytes 4194320 | tf_op jit(solution)/shard_map/psum | solution.py:134
  1114.3 13.9 %all-reduce.2 = (bf16[2048]{0:T(1024)(128)(2,1)S(1)}, bf16[2048]{0:T(1024)(128)(2,1)S(1)}) all-reduce(bf16[2048]{0:T(1024)(128)(2,1)S(1)} %get-tuple-element.64, bf16[2048]{0:T(1024)(128)(2,1)S(1)} %get-tuple-element.62), channel_id=6, replica_groups=mesh['dp'=4,'ctx'=2,'tensor'=4] {'dp','ctx'}, use_global_device_ids=true, to_apply=%region_16.17.clone | all-reduce | flops 4096 | bytes 16384
  1128.2 7.8 fusion.29
  (159 shorter events, 114.2 us)
Async XLA Ops:
  7.2 46.4 %copy-start = (bf16[512,2048]{1,0:T(8,128)(2,1)S(1)}, bf16[512,2048]{1,0:T(8,128)(2,1)}, u32[]{:S(2)}) copy-start(bf16[512,2048]{1,0:T(8,128)(2,1)} %param.18) | copy-start | bytes 6291460
  7.2 10.8 copy-start.20
  7.2 10.8 copy-start.14
  7.2 207.3 %all-reduce.7.cloned.1.call-start = ((), (), s32[]{:S(2)}) async-start(), calls=%async_computation.9 | async-start | bytes 8388608 | tf_op jit(solution)/shard_map/psum | solution.py:123
  56.8 161.2 %copy-start.19 = (f32[2048]{0:T(1024)S(1)}, f32[2048]{0:T(1024)}, u32[]{:S(2)}) copy-start(f32[2048]{0:T(1024)} %param.19) | copy-start | bytes 24580
  56.9 480.9 %all-gather.4.cloned.1.call-start = ((), (), s32[]{:S(2)}) async-start(), calls=%async_computation.19 | async-start | bytes 20971520 | tf_op jit(solution)/shard_map/all_gather | solution.py:149
  218.0 10.6 copy-start.2
  218.0 10.6 slice-start.4
  218.5 10.2 copy-start.8
  218.5 15.2 %slice-start.8 = ((s8[5767168]{0:T(1024)(128)(4,1)}), s8[4194304]{0:T(1024)(128)(4,1)S(1)}, s32[]{:S(2)}) async-start(s8[5767168]{0:T(1024)(128)(4,1)} %bitcast.216), calls=%async_computation.29 | async-start | bytes 8388608
  228.7 18.0 %slice-start.6 = ((s8[5767168]{0:T(1024)(128)(4,1)}), s8[4194304]{0:T(1024)(128)(4,1)S(1)}, s32[]{:S(2)}) async-start(s8[5767168]{0:T(1024)(128)(4,1)} %bitcast.214), calls=%async_computation.27 | async-start | bytes 8388608
  233.7 12.9 %slice-start.7 = ((s8[5767168]{0:T(1024)(128)(4,1)}), s8[1572864]{0:T(1024)(128)(4,1)S(1)}, s32[]{:S(2)}) async-start(s8[5767168]{0:T(1024)(128)(4,1)} %bitcast.214), calls=%async_computation.28 | async-start | bytes 3145728
  251.9 364.9 %reduce-scatter.12.cloned.1.call-start = ((), (), s32[]{:S(2)}) async-start(), calls=%async_computation.11 | async-start | bytes 393216 | tf_op jit(solution)/shard_map/reduce_scatter | solution.py:202
  548.0 13.3 %slice-start = ((s8[16777216]{0:T(1024)(128)(4,1)}), s8[4194304]{0:T(1024)(128)(4,1)S(1)}, s32[]{:S(2)}) async-start(s8[16777216]{0:T(1024)(128)(4,1)} %bitcast.192), calls=%async_computation.21 | async-start | bytes 8388608
  548.0 13.3 %slice-start.1 = ((s8[16777216]{0:T(1024)(128)(4,1)}), s8[4194304]{0:T(1024)(128)(4,1)S(1)}, s32[]{:S(2)}) async-start(s8[16777216]{0:T(1024)(128)(4,1)} %bitcast.192), calls=%async_computation.22 | async-start | bytes 8388608
  575.6 45.4 %reduce-scatter.10.cloned.1.call-start = ((), (), s32[]{:S(2)}) async-start(), calls=%async_computation.10 | async-start | bytes 393216 | tf_op jit(solution)/shard_map/reduce_scatter | solution.py:201
  594.4 69.9 %reduce-scatter.24.cloned.1.call-start = ((), (), s32[]{:S(2)}) async-start(), calls=%async_computation.17 | async-start | bytes 6488064 | tf_op jit(solution)/shard_map/reduce_scatter | solution.py:254
  601.5 125.2 %reduce-scatter.22.cloned.1.call-start = ((), (), s32[]{:S(2)}) async-start(), calls=%async_computation.16 | async-start | bytes 6488064 | tf_op jit(solution)/shard_map/reduce_scatter | solution.py:251
  608.3 181.3 %reduce-scatter.26.cloned.1.call-start = ((), (), s32[]{:S(2)}) async-start(), calls=%async_computation.18 | async-start | bytes 6488064 | tf_op jit(solution)/shard_map/reduce_scatter | solution.py:257
  616.7 209.6 %reduce-scatter.18.cloned.1.call-start = ((), (), s32[]{:S(2)}) async-start(), calls=%async_computation.14 | async-start | bytes 294912 | tf_op jit(solution)/shard_map/reduce_scatter | solution.py:242
  620.9 242.9 %reduce-scatter.16.cloned.1.call-start = ((), (), s32[]{:S(2)}) async-start(), calls=%async_computation.13 | async-start | bytes 294912 | tf_op jit(solution)/shard_map/reduce_scatter | solution.py:239
  623.7 284.5 %reduce-scatter.20.cloned.1.call-start = ((), (), s32[]{:S(2)}) async-start(), calls=%async_computation.15 | async-start | bytes 2359296 | tf_op jit(solution)/shard_map/reduce_scatter | solution.py:245
  628.5 324.6 %reduce-scatter.14.cloned.1.call-start = ((), (), s32[]{:S(2)}) async-start(), calls=%async_computation.12 | async-start | bytes 2359296 | tf_op jit(solution)/shard_map/reduce_scatter | solution.py:236
  636.9 474.5 %all-reduce.9.cloned.1.call-start = ((), (), s32[]{:S(2)}) async-start(), calls=%async_computation.20 | async-start | bytes 8388608 | tf_op jit(solution)/shard_map/psum | solution.py:134
  (22 other events, 99.8 us)
Sparse Core Ops, SparseCore 0:
  57.0 157.5 all-reduce.6
  252.0 285.7 all-gather.3
  575.7 5.8 reduce-scatter.11
  594.5 5.8 reduce-scatter.9
  604.1 60.1 reduce-scatter.23
  667.6 59.0 reduce-scatter.21
  730.6 59.0 reduce-scatter.25
  792.7 33.6 reduce-scatter.17
  830.2 33.6 reduce-scatter.15
  867.0 41.1 reduce-scatter.19
  911.9 41.2 reduce-scatter.13
  956.0 155.3 all-reduce.8
